TPU v7x, 256 devices: a whole 4x4x8 slice. The times are simulated.
256 devices in a mesh: spec: 16 (over z_lo, x, core), photo: 16 (over y, z_hi).
Axes of the slice: x: 4, y: 4, z: 8 (z_hi: 4, z_lo: 2; z = z_hi * 2 + z_lo), core: 2. Of those that a mesh axis runs over, the one named last changes fastest.
Arguments:
- spec_feat: bfloat16 [131072, 64], P(('spec', 'photo')), may hold values from -2.5 to 2.5
- photo_feat: bfloat16 [16, 16384, 64], P('spec', 'photo'), may hold values from -2.5 to 2.5
- spec_mass: bfloat16 [131072], P(('spec', 'photo')), may hold values from 0.25 to 4
- photo_mass: bfloat16 [16, 16384], P('spec', 'photo'), may hold values from 0.25 to 4
- tile_index: int32 [16, 16, 96], P('spec', 'photo'), may hold values from 0 to 2047, as said below
- tile_count: int32 [16, 16], P('spec', 'photo'), may hold values from 4 to 96, as said below
Outputs:
- grad_spec: float32 [131072, 64], P(('spec', 'photo'))
- grad_photo: float32 [16, 16384, 64], P('spec', 'photo')
Inputs may be any that keep to these rules, and one draw needn't show every extreme that they name: `tile_index`: the first tile_count[s, p] entries of each list are distinct; over all lists, every tile row of every spectroscopic block and every tile column of every photometric block lies in some live tile. Entries past the count are ignored. `tile_count`: some pair of blocks has exactly 96 live tiles.
All inputs are finite; a program needn't handle non-finite values.
Results may differ from a plain program's by a relative error of at most 0.002.
Values may be sent and summed in bfloat16 or wider, within the bound.
No kernel may reach another device: no remote copies, remote signals or barrier semaphores. Data moves between devices by JAX's collectives and lax.ppermute only.
A program may use at most 64 MiB of HBM per device.

v0:
```python
import jax
import jax.numpy as jnp
from jax import lax
from jax.sharding import PartitionSpec as P

TILE = 256
SWEEPS = 2
TEMPER = 16.0
GROUP = 8


def per_device(spec_feat, photo_feat, spec_mass, photo_mass, tile_index, tile_count):
    spec_rows, spec_weights = (
        lax.all_gather(spec_feat, "photo", axis=0, tiled=True),
        lax.all_gather(spec_mass, "photo", axis=0, tiled=True),
    )
    photo_rows, photo_weights = (
        lax.all_gather(photo_feat, "spec", axis=0, tiled=True),
        lax.all_gather(photo_mass, "spec", axis=0, tiled=True),
    )
    feat_width = spec_rows.shape[1]
    spec_count = spec_rows.shape[0]
    photo_count = photo_rows.shape[0] * photo_rows.shape[1]
    tile_rows = spec_count // TILE
    tile_cols = photo_count // TILE
    share_len = photo_feat.shape[1]
    spec_blocks = spec_rows.reshape(tile_rows, TILE, feat_width)
    photo_blocks = photo_rows.reshape(tile_cols, TILE, feat_width)
    spec_squares = jnp.sum(jnp.square(spec_blocks.astype(jnp.float32)), axis=2)
    photo_squares = jnp.sum(jnp.square(photo_blocks.astype(jnp.float32)), axis=2)
    slots = tile_index.reshape(-1)
    count = tile_count.reshape(())
    turns = (count + GROUP - 1) // GROUP

    def tile_group(group):
        first = group * GROUP
        picked = lax.dynamic_slice_in_dim(slots, first, GROUP)
        live = first + jnp.arange(GROUP, dtype=jnp.int32) < count
        rows = picked // tile_cols
        columns = picked % tile_cols
        spec_tiles = spec_blocks[rows]
        photo_tiles = photo_blocks[columns]
        cross = jnp.einsum(
            "gif,gjf->gij", spec_tiles, photo_tiles, preferred_element_type=jnp.float32
        )
        dist = spec_squares[rows][:, :, None] + photo_squares[columns][:, None, :] - 2.0 * cross
        kernel = jnp.where(live[:, None, None], jnp.exp(-dist / TEMPER), jnp.float32(0.0))
        return (rows, columns, spec_tiles, photo_tiles, kernel)

    column_scale = jnp.ones((tile_cols, TILE), jnp.float32)
    row_scale = jnp.ones((tile_rows, TILE), jnp.float32)
    marginal_share = jnp.zeros((share_len,), jnp.float32)
    for sweep in range(SWEEPS):

        def row_step(group, total):
            rows, columns, spec_tiles, photo_tiles, kernel = tile_group(group)
            sums = jnp.sum(kernel * column_scale[columns][:, None, :], axis=2)
            return total.at[rows].add(sums)

        row_part = lax.fori_loop(0, turns, row_step, jnp.zeros((tile_rows, TILE), jnp.float32))
        row_total = lax.psum(row_part, "photo")
        row_scale = spec_weights.astype(jnp.float32).reshape(tile_rows, TILE) / row_total

        def column_step(group, total):
            rows, columns, spec_tiles, photo_tiles, kernel = tile_group(group)
            sums = jnp.sum(row_scale[rows][:, :, None] * kernel, axis=1)
            return total.at[columns].add(sums)

        column_part = lax.fori_loop(
            0, turns, column_step, jnp.zeros((tile_cols, TILE), jnp.float32)
        )
        column_total = lax.psum(column_part, "spec")
        column_scale = photo_weights.astype(jnp.float32).reshape(tile_cols, TILE) / column_total
        marginal = (column_scale * column_total).reshape(-1)
        marginal_share = lax.dynamic_slice_in_dim(
            marginal, lax.axis_index("spec") * share_len, share_len
        )

    def plan_tiles(rows, columns, kernel):
        plan = row_scale[rows][:, :, None] * kernel * column_scale[columns][:, None, :]
        return (plan, plan.astype(jnp.bfloat16))

    def grad_step(group, carry):
        row_sum, spec_acc, photo_acc = carry
        rows, columns, spec_tiles, photo_tiles, kernel = tile_group(group)
        plan, plan_low = plan_tiles(rows, columns, kernel)
        row_sum = row_sum.at[rows].add(jnp.sum(plan, axis=2))
        toward = jnp.einsum(
            "gij,gjf->gif", plan_low, photo_tiles, preferred_element_type=jnp.float32
        ).reshape(GROUP, -1)
        spec_acc = spec_acc.at[rows].add(toward)
        back = jnp.einsum(
            "gij,gif->gjf", plan_low, spec_tiles, preferred_element_type=jnp.float32
        ).reshape(GROUP, -1)
        photo_acc = photo_acc.at[columns].add(back)
        return (row_sum, spec_acc, photo_acc)

    start = (
        jnp.zeros((tile_rows, TILE), jnp.float32),
        jnp.zeros((tile_rows, TILE * feat_width), jnp.float32),
        jnp.zeros((tile_cols, TILE * feat_width), jnp.float32),
    )
    row_sum, spec_acc, photo_acc = lax.fori_loop(0, turns, grad_step, start)
    pulled = spec_acc.reshape(spec_count, feat_width)
    row_marginal = lax.psum(row_sum, "photo")
    spec_term = -2.0 * pulled
    spec_share = lax.psum_scatter(
        spec_term.astype(jnp.bfloat16), "photo", scatter_dimension=0, tiled=True
    ).astype(jnp.float32)
    own_rows = spec_feat.shape[0]
    marginal_rows = lax.dynamic_slice_in_dim(
        row_marginal.reshape(-1), lax.axis_index("photo") * own_rows, own_rows
    )
    spec_share = spec_share + 2.0 * marginal_rows[:, None] * spec_feat.astype(jnp.float32)
    photo_term = -2.0 * photo_acc.reshape(photo_count, feat_width)
    photo_share = lax.psum_scatter(photo_term, "spec", scatter_dimension=0, tiled=True)
    photo_share = photo_share + 2.0 * marginal_share[:, None] * photo_feat[0].astype(jnp.float32)
    return (spec_share, photo_share[None])


def solution(mesh):
    return jax.shard_map(
        per_device,
        mesh=mesh,
        in_specs=(
            P(("spec", "photo"), None),
            P("spec", "photo", None),
            P(("spec", "photo")),
            P("spec", "photo"),
            P("spec", "photo", None),
            P("spec", "photo"),
        ),
        out_specs=(P(("spec", "photo"), None), P("spec", "photo", None)),
        check_vma=False,
    )
```

profile of v0, /device:TPU:8, one launch (start us, length us, event | category | flops | bytes accessed | tf_op | source)
XLA Modules:
  0.0 1373.2 jit_solution(6918769820920343711)
XLA Ops:
  10.0 41.3 %all-gather = bf16[16,1,512]{2,1,0:T(2,128)(2,1)S(1)} all-gather(bf16[1,1,512]{2,1,0:T(2,128)(2,1)S(1)} %reshape.416), channel_id=1, replica_groups=mesh['spec'=16,'photo'=16] {'photo'}, dimensions={0}, use_global_device_ids=true | all-gather | bytes 17408 | tf_op jit(solution)/shard_map/all_gather | solution.py:15
  51.5 19.6 %all-gather.1 = bf16[16,1,1024]{2,1,0:T(2,128)(2,1)S(1)} all-gather(bf16[1,1,1024]{2,1,0:T(2,128)(2,1)} %bitcast.64), channel_id=1, replica_groups=mesh['spec'=16,'photo'=16] {'spec'}, dimensions={0}, use_global_device_ids=true | all-gather | bytes 34816 | tf_op jit(solution)/shard_map/all_gather | solution.py:19
  71.1 1.5 multiply_reduce_fusion.5
  72.6 2.0 copy.83
  74.6 28.7 %all-gather.7.cloned.1.call-done = bf16[16,1024,64]{1,2,0:T(8,128)(2,1)} async-done(((bf16[1,1024,64]{1,2,0:T(8,128)(2,1)}), bf16[16,1024,64]{1,2,0:T(8,128)(2,1)}) %all-gather.7.cloned.1.call-update) | async-done | bytes 2097168 | tf_op jit(solution)/shard_map/all_gather | solution.py:18
  103.3 2.1 multiply_reduce_fusion.4
  105.5 4.8 copy.110
  110.3 23.4 %while.64 = (s32[]{:T(128)}, f32[32,256]{1,0:T(8,128)S(1)}, s32[]{:T(128)}, s32[96]{0:T(128)S(1)}, s32[]{:T(128)}, /*index=5*/f32[32,256]{1,0:T(8,128)S(1)}, f32...) while((s32[]{:T(128)}, f32[32,256]{1,0:T(8,128)S(1)}, ...), condition=%wide.region_5.6_spmd, body=%wide.region_2.5_spmd.sunk | while | flops 71305472 | bytes 1753751 | solution.py:60
  111.7 2.8 gather_fusion.1
  119.5 2.8 gather_fusion.1
  127.3 2.8 gather_fusion.1
  133.7 130.7 %psum.35 = f32[32,256]{1,0:T(8,128)S(1)} all-reduce(f32[32,256]{1,0:T(8,128)S(1)} %get-tuple-element.683), channel_id=1, replica_groups=mesh['spec'=16,'photo'=16] {'photo'}, use_global_device_ids=true, to_apply=%region_6.7 | all-reduce | flops 8192 | bytes 65536 | tf_op jit(solution)/shard_map/psum | solution.py:61
  264.4 23.2 %while.65 = (s32[]{:T(128)}, f32[64,256]{1,0:T(8,128)S(1)}, s32[]{:T(128)}, s32[96]{0:T(128)S(1)}, f32[32,256]{1,0:T(8,128)S(1)}, /*index=5*/s32[]{:T(128)}, f32...) while((s32[]{:T(128)}, f32[64,256]{1,0:T(8,128)S(1)}, ...), condition=%wide.region_10.11_spmd, body=%wide.region_7.10_spmd.sunk | while | flops 71305448 | bytes 1688175 | solution.py:69
  264.6 2.8 gather_fusion.6
  272.3 2.8 gather_fusion.6
  280.0 2.8 gather_fusion.6
  288.6 192.6 %all-reduce.3.cloned.1.call-done = f32[64,256]{1,0:T(8,128)} async-done(((f32[64,256]{1,0:T(8,128)}), f32[64,256]{1,0:T(8,128)}) %all-reduce.3.cloned.1.call-update) | async-done | bytes 65552 | tf_op jit(solution)/shard_map/psum | solution.py:72
  482.0 23.4 %while.66 = (s32[]{:T(128)}, f32[32,256]{1,0:T(8,128)S(1)}, s32[]{:T(128)}, s32[96]{0:T(128)S(1)}, s32[]{:T(128)}, /*index=5*/f32[32,256]{1,0:T(8,128)S(1)}, f32...) while((s32[]{:T(128)}, f32[32,256]{1,0:T(8,128)S(1)}, ...), condition=%wide.region_15.16_spmd, body=%wide.region_12.15_spmd.sunk | while | flops 71305472 | bytes 1688211 | solution.py:60
  483.5 2.8 gather_fusion.11
  491.3 2.8 gather_fusion.11
  499.0 2.8 gather_fusion.11
  505.4 131.4 %psum.37 = f32[32,256]{1,0:T(8,128)S(1)} all-reduce(f32[32,256]{1,0:T(8,128)S(1)} %get-tuple-element.685), channel_id=1, replica_groups=mesh['spec'=16,'photo'=16] {'photo'}, use_global_device_ids=true, to_apply=%region_16.17 | all-reduce | flops 8192 | bytes 65536 | tf_op jit(solution)/shard_map/psum | solution.py:61
  636.8 23.2 %while.67 = (s32[]{:T(128)}, f32[64,256]{1,0:T(8,128)S(1)}, s32[]{:T(128)}, s32[96]{0:T(128)S(1)}, f32[32,256]{1,0:T(8,128)S(1)}, /*index=5*/s32[]{:T(128)}, f32...) while((s32[]{:T(128)}, f32[64,256]{1,0:T(8,128)S(1)}, ...), condition=%wide.region_20.21_spmd, body=%wide.region_17.20_spmd.sunk | while | flops 71305448 | bytes 1688175 | solution.py:69
  636.9 2.8 gather_fusion.16
  644.7 2.8 gather_fusion.16
  650.5 1.0 multiply_reduce_fusion.13
  652.4 2.8 gather_fusion.16
  660.7 191.8 %all-reduce.5.cloned.1.call-done = f32[64,256]{1,0:T(8,128)} async-done(((f32[64,256]{1,0:T(8,128)}), f32[64,256]{1,0:T(8,128)}) %all-reduce.5.cloned.1.call-update) | async-done | bytes 65552 | tf_op jit(solution)/shard_map/psum | solution.py:72
  853.4 2.3 broadcast_in_dim.201
  855.8 84.9 %while.68 = (s32[]{:T(128)}, f32[32,256]{1,0:T(8,128)S(1)}, f32[32,16384]{1,0:T(8,128)S(1)}, f32[64,16384]{1,0:T(8,128)}, s32[]{:T(128)}, /*index=5*/s32[96]{0:T...) while((s32[]{:T(128)}, f32[32,256]{1,0:T(8,128)S(1)}, ...), condition=%wide.region_27.28_spmd, body=%wide.region_22.27_spmd.sunk | while | flops 206833920 | bytes 12722983 | solution.py:103
  856.2 3.0 gather_fusion.21
  860.4 3.6 gather_fusion.22
  865.8 2.2 fusion.52
  868.0 1.4 fusion.54
  869.4 2.4 reshape.565
  871.8 5.8 scatter_fusion.6
  877.5 2.5 fusion.53
  880.0 1.6 reshape.564
  881.6 1.9 scatter_fusion.5
  884.5 3.0 gather_fusion.21
  888.6 3.6 gather_fusion.22
  894.0 2.2 fusion.52
  896.2 1.4 fusion.54
  897.6 2.4 reshape.565
  900.0 5.8 scatter_fusion.6
  905.8 2.5 fusion.53
  908.3 1.6 reshape.564
  909.9 1.9 scatter_fusion.5
  912.7 3.0 gather_fusion.21
  916.9 3.6 gather_fusion.22
  922.3 2.2 fusion.52
  924.5 1.4 fusion.54
  925.9 2.4 reshape.565
  928.3 5.8 scatter_fusion.6
  934.0 2.5 fusion.53
  936.6 1.6 reshape.564
  938.1 1.9 scatter_fusion.5
  940.9 3.3 convert_element_type.39
  944.2 4.5 broadcast_multiply_fusion
  948.7 7.4 mul.208
  957.4 295.6 %psum.39 = f32[8192]{0:T(1024)S(1)} all-reduce(f32[8192]{0:T(1024)S(1)} %bitcast.62), channel_id=1, replica_groups=mesh['spec'=16,'photo'=16] {'photo'}, use_global_device_ids=true, to_apply=%region_29.30 | all-reduce | flops 8192 | bytes 65536 | tf_op jit(solution)/shard_map/psum | solution.py:105
  1253.1 32.7 %reduce-scatter.3.cloned.1.call-done = bf16[512,64]{1,0:T(8,128)(2,1)} async-done(((bf16[8192,64]{1,0:T(8,128)(2,1)}), bf16[512,64]{1,0:T(8,128)(2,1)}) %reduce-scatter.3.cloned.1.call-update) | async-done | bytes 65552 | tf_op jit(solution)/shard_map/reduce_scatter | solution.py:107
  1287.5 76.6 %reduce-scatter.5.cloned.1.call-done = f32[1024,64]{1,0:T(8,128)} async-done(((f32[16384,64]{1,0:T(8,128)}), f32[1024,64]{1,0:T(8,128)}) %reduce-scatter.5.cloned.1.call-update) | async-done | bytes 262160 | tf_op jit(solution)/shard_map/reduce_scatter | solution.py:116
  1364.2 1.2 fusion.5
  (222 shorter events, 78.4 us)
Async XLA Ops:
  7.2 63.9 %all-gather.5.cloned.1.call-start = ((), (), s32[]{:S(2)}) async-start(), calls=%async_computation.2 | async-start | bytes 1114112 | tf_op jit(solution)/shard_map/all_gather | solution.py:14
  7.9 95.4 %all-gather.7.cloned.1.call-start = ((), (), s32[]{:S(2)}) async-start(), calls=%async_computation.3 | async-start | bytes 2228224 | tf_op jit(solution)/shard_map/all_gather | solution.py:18
  8.6 472.5 %all-reduce.3.cloned.1.call-start = ((), (), s32[]{:S(2)}) async-start(), calls=%async_computation.4 | async-start | bytes 131072 | tf_op jit(solution)/shard_map/psum | solution.py:72
  105.5 4.8 copy-start.4
  287.7 0.6 copy-start.2
  288.3 564.2 %all-reduce.5.cloned.1.call-start = ((), (), s32[]{:S(2)}) async-start(), calls=%async_computation.5 | async-start | bytes 131072 | tf_op jit(solution)/shard_map/psum | solution.py:72
  660.0 0.6 copy-start.3
  660.0 193.3 %copy-start = (bf16[32,256,64]{2,1,0:T(8,128)(2,1)}, bf16[32,256,64]{2,1,0:T(8,128)(2,1)S(1)}, u32[]{:S(2)}) copy-start(bf16[32,256,64]{2,1,0:T(8,128)(2,1)S(1)} %get-tuple-element.1442) | copy-start | bytes 3145732
  660.7 625.0 %reduce-scatter.3.cloned.1.call-start = ((), (), s32[]{:S(2)}) async-start(), calls=%async_computation.6 | async-start | bytes 2228224 | tf_op jit(solution)/shard_map/reduce_scatter | solution.py:107
  865.8 2.2 copy-start.1
  894.0 2.2 copy-start.1
  922.3 2.2 copy-start.1
  944.2 420.0 %reduce-scatter.5.cloned.1.call-start = ((), (), s32[]{:S(2)}) async-start(), calls=%async_computation.7 | async-start | bytes 8912896 | tf_op jit(solution)/shard_map/reduce_scatter | solution.py:116
  956.1 0.9 copy-start.5
  956.1 1.1 copy-start.6
Sparse Core Ops, SparseCore 0:
  10.4 55.9 all-gather.4
  68.2 35.0 all-gather.6
  288.4 192.6 all-reduce.2
  660.8 191.6 all-reduce.4
  944.3 341.3 reduce-scatter.2
  1288.1 76.0 reduce-scatter.4
where the time goes:
time: 1380 us; the launch traced here: 1370 us
  blocking collectives  619 us (45%)
  waiting for transfers between devices  524 us (38%)
  local copies, waits for them, and re-layouts  125 us (9%)
  other arithmetic  58.2 us (4%)
  matrix products  30.5 us (2%)
  between operations  15 us (1%)
    psum x2, waiting for transfers between devices, per_device(): column_total = lax.psum(column_part, 'spec')  384 us
    psum x1, blocking collectives, per_device(): row_marginal = lax.psum(row_sum, 'photo')  296 us
    psum x2, blocking collectives, per_device(): row_total = lax.psum(row_part, 'photo')  262 us
    reduce_scatter x1, waiting for transfers between devices, per_device(): lax.psum_scatter(photo_term, 'spec', scatter_dimension=0, tiled=True)  76.6 us
    gather x15, local copies, waits for them, and re-layouts, tile_group(): photo_tiles = photo_blocks[columns]  44.8 us
    all_gather x1, blocking collectives, per_device(): lax.all_gather(spec_mass, 'photo', axis=0, tiled=True)  41.3 us
    reduce_scatter x1, waiting for transfers between devices, per_device(): lax.psum_scatter(spec_term.astype(jnp.bfloat16), 'photo', scatter_dimensi...  32.7 us
    all_gather x1, waiting for transfers between devices, per_device(): lax.all_gather(photo_feat, 'spec', axis=0, tiled=True)  28.7 us
  transfers between devices with their start and end apart: 6, of which 5 were waited for; matrix products, arithmetic and copies ran while one was open for 1% of the time, Pallas kernels for 0%

commit v1 on v0

--- a/solution.py
+++ b/solution.py
@@ -69,7 +69,8 @@
         column_part = lax.fori_loop(
             0, turns, column_step, jnp.zeros((tile_cols, TILE), jnp.float32)
         )
-        column_total = lax.psum(column_part, "spec")
+        shards = lax.all_gather(column_part, "spec", axis=0, tiled=False)
+        column_total = shards.sum(axis=0)
         column_scale = photo_weights.astype(jnp.float32).reshape(tile_cols, TILE) / column_total
         marginal = (column_scale * column_total).reshape(-1)
         marginal_share = lax.dynamic_slice_in_dim(

time: 1380 us -> 1230 us (0.89)
  waiting for transfers between devices: 524 us -> 315 us
  blocking collectives: 619 us -> 673 us
    psum x2 -> x0, waiting for transfers between devices: 384 us -> none  [per_device(): column_total = lax.psum(column_part, 'spec')]
    all_gather x0 -> x2, waiting for transfers between devices: none -> 155 us  [per_device(): shards = lax.all_gather(column_part, 'spec', axis=0, tiled=False)]
    all_gather x1, blocking collectives: 19.6 us -> 74.6 us  [per_device(): lax.all_gather(photo_mass, 'spec', axis=0, tiled=True)]
    all_gather x1, waiting for transfers between devices: 0.01 us -> 14.9 us  [per_device(): lax.all_gather(spec_feat, 'photo', axis=0, tiled=True)]
  transfers between devices with their start and end apart: 6 -> 6, of which waited for: 5 -> 6; matrix products, arithmetic and copies ran while one was open for 1% -> 2% of each run, Pallas kernels for 0% -> 0%
where the time goes in v1:
time: 1230 us; the launch traced here: 1220 us
  blocking collectives  673 us (55%)
  waiting for transfers between devices  315 us (26%)
  local copies, waits for them, and re-layouts  125 us (10%)
  other arithmetic  59.1 us (5%)
  matrix products  30.5 us (2%)
  between operations  15.1 us (1%)
    psum x1, blocking collectives, per_device(): row_marginal = lax.psum(row_sum, 'photo')  295 us
    psum x2, blocking collectives, per_device(): row_total = lax.psum(row_part, 'photo')  262 us
    all_gather x2, waiting for transfers between devices, per_device(): shards = lax.all_gather(column_part, 'spec', axis=0, tiled=False)  155 us
    reduce_scatter x1, waiting for transfers between devices, per_device(): lax.psum_scatter(photo_term, 'spec', scatter_dimension=0, tiled=True)  76.6 us
    all_gather x1, blocking collectives, per_device(): lax.all_gather(photo_mass, 'spec', axis=0, tiled=True)  74.6 us
    gather x15, local copies, waits for them, and re-layouts, tile_group(): photo_tiles = photo_blocks[columns]  44.8 us
    all_gather x1, blocking collectives, per_device(): lax.all_gather(spec_mass, 'photo', axis=0, tiled=True)  41.3 us
    reduce_scatter x1, waiting for transfers between devices, per_device(): lax.psum_scatter(spec_term.astype(jnp.bfloat16), 'photo', scatter_dimensi...  33.8 us
  transfers between devices with their start and end apart: 6, of which 6 were waited for; matrix products, arithmetic and copies ran while one was open for 2% of the time, Pallas kernels for 0%

profile of v1, /device:TPU:8, one launch (start us, length us, event | category | flops | bytes accessed | tf_op | source)
XLA Modules:
  0.0 1219.2 jit_solution(11327606068624133590)
XLA Ops:
  10.0 41.3 %all-gather.2 = bf16[16,1,512]{2,1,0:T(2,128)(2,1)S(1)} all-gather(bf16[1,1,512]{2,1,0:T(2,128)(2,1)S(1)} %reshape.414), channel_id=1, replica_groups=mesh['spec'=16,'photo'=16] {'photo'}, dimensions={0}, use_global_device_ids=true | all-gather | bytes 17408 | tf_op jit(solution)/shard_map/all_gather | solution.py:15
  51.5 14.9 %all-gather.9.cloned.1.call-done = bf16[8192,64]{0,1:T(8,128)(2,1)} async-done(((bf16[512,64]{0,1:T(8,128)(2,1)}), bf16[8192,64]{0,1:T(8,128)(2,1)}) %all-gather.9.cloned.1.call-update) | async-done | bytes 1048592 | tf_op jit(solution)/shard_map/all_gather | solution.py:14
  66.4 1.5 multiply_reduce_fusion.5
  67.9 2.0 copy.83
  69.9 32.9 %all-gather.11.cloned.1.call-done = bf16[16,1024,64]{1,2,0:T(8,128)(2,1)} async-done(((bf16[1,1024,64]{1,2,0:T(8,128)(2,1)}), bf16[16,1024,64]{1,2,0:T(8,128)(2,1)}) %all-gather.11.cloned.1.call-update) | async-done | bytes 2097168 | tf_op jit(solution)/shard_map/all_gather | solution.py:18
  102.9 2.1 multiply_reduce_fusion.4
  105.0 4.8 copy.110
  109.8 23.4 %while.64 = (s32[]{:T(128)}, f32[32,256]{1,0:T(8,128)S(1)}, s32[]{:T(128)}, s32[96]{0:T(128)S(1)}, s32[]{:T(128)}, /*index=5*/f32[32,256]{1,0:T(8,128)S(1)}, f32...) while((s32[]{:T(128)}, f32[32,256]{1,0:T(8,128)S(1)}, ...), condition=%wide.region_5.6_spmd, body=%wide.region_2.5_spmd.sunk | while | flops 71305472 | bytes 1753751 | solution.py:60
  111.2 2.8 gather_fusion.1
  119.0 2.8 gather_fusion.1
  126.8 2.8 gather_fusion.1
  133.2 130.7 %psum.21 = f32[32,256]{1,0:T(8,128)S(1)} all-reduce(f32[32,256]{1,0:T(8,128)S(1)} %get-tuple-element.683), channel_id=1, replica_groups=mesh['spec'=16,'photo'=16] {'photo'}, use_global_device_ids=true, to_apply=%region_6.7 | all-reduce | flops 8192 | bytes 65536 | tf_op jit(solution)/shard_map/psum | solution.py:61
  264.0 23.2 %while.65 = (s32[]{:T(128)}, f32[64,256]{1,0:T(8,128)S(1)}, s32[]{:T(128)}, s32[96]{0:T(128)S(1)}, f32[32,256]{1,0:T(8,128)S(1)}, /*index=5*/s32[]{:T(128)}, f32...) while((s32[]{:T(128)}, f32[64,256]{1,0:T(8,128)S(1)}, ...), condition=%wide.region_10.11_spmd, body=%wide.region_7.10_spmd.sunk | while | flops 71305448 | bytes 1688175 | solution.py:69
  264.1 2.8 gather_fusion.6
  271.9 2.8 gather_fusion.6
  279.6 2.8 gather_fusion.6
  287.9 74.6 %all-gather.3 = bf16[16,1,1024]{2,1,0:T(2,128)(2,1)S(1)} all-gather(bf16[1,1,1024]{2,1,0:T(2,128)(2,1)S(1)} %bitcast.70), channel_id=1, replica_groups=mesh['spec'=16,'photo'=16] {'spec'}, dimensions={0}, use_global_device_ids=true | all-gather | bytes 34816 | tf_op jit(solution)/shard_map/all_gather | solution.py:19
  362.8 40.2 %all-gather.13.cloned.1.call-done = f32[1024,256]{1,0:T(8,128)} async-done(((f32[64,256]{1,0:T(8,128)}), f32[1024,256]{1,0:T(8,128)}) %all-gather.13.cloned.1.call-update) | async-done | bytes 1048592 | tf_op jit(solution)/shard_map/all_gather | solution.py:72
  403.0 1.3 reduce_sum.106
  404.3 23.4 %while.66 = (s32[]{:T(128)}, f32[32,256]{1,0:T(8,128)S(1)}, s32[]{:T(128)}, s32[96]{0:T(128)S(1)}, s32[]{:T(128)}, /*index=5*/f32[32,256]{1,0:T(8,128)S(1)}, f32...) while((s32[]{:T(128)}, f32[32,256]{1,0:T(8,128)S(1)}, ...), condition=%wide.region_15.16_spmd, body=%wide.region_12.15_spmd.sunk | while | flops 71305472 | bytes 1688211 | solution.py:60
  405.8 2.8 gather_fusion.11
  413.6 2.8 gather_fusion.11
  421.4 2.8 gather_fusion.11
  427.7 130.9 %psum.22 = f32[32,256]{1,0:T(8,128)S(1)} all-reduce(f32[32,256]{1,0:T(8,128)S(1)} %get-tuple-element.685), channel_id=1, replica_groups=mesh['spec'=16,'photo'=16] {'photo'}, use_global_device_ids=true, to_apply=%region_16.17 | all-reduce | flops 8192 | bytes 65536 | tf_op jit(solution)/shard_map/psum | solution.py:61
  558.6 23.2 %while.67 = (s32[]{:T(128)}, f32[64,256]{1,0:T(8,128)S(1)}, s32[]{:T(128)}, s32[96]{0:T(128)S(1)}, f32[32,256]{1,0:T(8,128)S(1)}, /*index=5*/s32[]{:T(128)}, f32...) while((s32[]{:T(128)}, f32[64,256]{1,0:T(8,128)S(1)}, ...), condition=%wide.region_20.21_spmd, body=%wide.region_17.20_spmd.sunk | while | flops 71305448 | bytes 1688175 | solution.py:69
  558.8 2.8 gather_fusion.16
  566.5 2.8 gather_fusion.16
  574.3 2.8 gather_fusion.16
  582.6 114.9 %all-gather.15.cloned.1.call-done = f32[1024,256]{1,0:T(8,128)} async-done(((f32[64,256]{1,0:T(8,128)}), f32[1024,256]{1,0:T(8,128)}) %all-gather.15.cloned.1.call-update) | async-done | bytes 1048592 | tf_op jit(solution)/shard_map/all_gather | solution.py:72
  698.9 2.3 broadcast_in_dim.201
  701.3 84.9 %while.68 = (s32[]{:T(128)}, f32[32,256]{1,0:T(8,128)S(1)}, f32[32,16384]{1,0:T(8,128)S(1)}, f32[64,16384]{1,0:T(8,128)}, s32[]{:T(128)}, /*index=5*/s32[96]{0:T...) while((s32[]{:T(128)}, f32[32,256]{1,0:T(8,128)S(1)}, ...), condition=%wide.region_27.28_spmd, body=%wide.region_22.27_spmd.sunk | while | flops 206833920 | bytes 12722983 | solution.py:104
  701.7 3.0 gather_fusion.21
  705.9 3.6 gather_fusion.22
  711.3 2.2 fusion.53
  713.4 1.4 fusion.55
  714.9 2.4 reshape.562
  717.2 5.8 scatter_fusion.6
  723.0 2.5 fusion.54
  725.5 1.6 reshape.561
  727.1 1.9 scatter_fusion.5
  730.0 3.0 gather_fusion.21
  734.1 3.6 gather_fusion.22
  739.5 2.2 fusion.53
  741.7 1.4 fusion.55
  743.1 2.4 reshape.562
  745.5 5.8 scatter_fusion.6
  751.3 2.5 fusion.54
  753.8 1.6 reshape.561
  755.4 1.9 scatter_fusion.5
  758.2 3.0 gather_fusion.21
  762.4 3.6 gather_fusion.22
  767.8 2.2 fusion.53
  770.0 1.4 fusion.55
  771.4 2.4 reshape.562
  773.8 5.8 scatter_fusion.6
  779.5 2.5 fusion.54
  782.0 1.6 reshape.561
  783.6 1.9 scatter_fusion.5
  786.4 3.3 convert_element_type.42
  789.7 4.5 broadcast_multiply_fusion
  794.2 7.4 mul.209
  802.9 295.1 %psum.23 = f32[8192]{0:T(1024)S(1)} all-reduce(f32[8192]{0:T(1024)S(1)} %bitcast.67), channel_id=1, replica_groups=mesh['spec'=16,'photo'=16] {'photo'}, use_global_device_ids=true, to_apply=%region_29.30 | all-reduce | flops 8192 | bytes 65536 | tf_op jit(solution)/shard_map/psum | solution.py:106
  1098.0 33.8 %reduce-scatter.3.cloned.1.call-done = bf16[512,64]{1,0:T(8,128)(2,1)} async-done(((bf16[8192,64]{1,0:T(8,128)(2,1)}), bf16[512,64]{1,0:T(8,128)(2,1)}) %reduce-scatter.3.cloned.1.call-update) | async-done | bytes 65552 | tf_op jit(solution)/shard_map/reduce_scatter | solution.py:108
  1133.6 76.6 %reduce-scatter.5.cloned.1.call-done = f32[1024,64]{1,0:T(8,128)} async-done(((f32[16384,64]{1,0:T(8,128)}), f32[1024,64]{1,0:T(8,128)}) %reduce-scatter.5.cloned.1.call-update) | async-done | bytes 262160 | tf_op jit(solution)/shard_map/reduce_scatter | solution.py:117
  (231 shorter events, 80.4 us)
Async XLA Ops:
  7.2 59.2 %all-gather.9.cloned.1.call-start = ((), (), s32[]{:S(2)}) async-start(), calls=%async_computation.2 | async-start | bytes 1114112 | tf_op jit(solution)/shard_map/all_gather | solution.py:14
  7.9 95.0 %all-gather.11.cloned.1.call-start = ((), (), s32[]{:S(2)}) async-start(), calls=%async_computation.3 | async-start | bytes 2228224 | tf_op jit(solution)/shard_map/all_gather | solution.py:18
  8.6 394.4 %all-gather.13.cloned.1.call-start = ((), (), s32[]{:S(2)}) async-start(), calls=%async_computation.6 | async-start | bytes 1114112 | tf_op jit(solution)/shard_map/all_gather | solution.py:72
  105.0 4.8 copy-start.4
  264.0 23.9 %copy-start.9 = (bf16[1,1024]{1,0:T(2,128)(2,1)S(1)}, bf16[1,1024]{1,0:T(2,128)(2,1)}, u32[]{:S(2)}) copy-start(bf16[1,1024]{1,0:T(2,128)(2,1)} %param.19) | copy-start | bytes 6148
  287.2 0.6 copy-start.2
  287.9 409.6 %all-gather.15.cloned.1.call-start = ((), (), s32[]{:S(2)}) async-start(), calls=%async_computation.7 | async-start | bytes 1114112 | tf_op jit(solution)/shard_map/all_gather | solution.py:72
  362.6 40.4 %copy-start.5 = (bf16[16,1,1024]{2,1,0:T(2,128)(2,1)}, bf16[16,1,1024]{2,1,0:T(2,128)(2,1)S(1)}, u32[]{:S(2)}) copy-start(bf16[16,1,1024]{2,1,0:T(2,128)(2,1)S(1)} %all-gather.3) | copy-start | bytes 98308
  581.9 0.6 copy-start.3
  581.9 117.0 %copy-start = (bf16[32,256,64]{2,1,0:T(8,128)(2,1)}, bf16[32,256,64]{2,1,0:T(8,128)(2,1)S(1)}, u32[]{:S(2)}) copy-start(bf16[32,256,64]{2,1,0:T(8,128)(2,1)S(1)} %get-tuple-element.1440) | copy-start | bytes 3145732
  582.5 549.3 %reduce-scatter.3.cloned.1.call-start = ((), (), s32[]{:S(2)}) async-start(), calls=%async_computation.4 | async-start | bytes 2228224 | tf_op jit(solution)/shard_map/reduce_scatter | solution.py:108
  711.3 2.2 copy-start.1
  739.5 2.2 copy-start.1
  767.8 2.2 copy-start.1
  789.7 420.6 %reduce-scatter.5.cloned.1.call-start = ((), (), s32[]{:S(2)}) async-start(), calls=%async_computation.5 | async-start | bytes 8912896 | tf_op jit(solution)/shard_map/reduce_scatter | solution.py:117
  801.6 0.8 copy-start.6
  801.6 0.9 copy-start.7
  801.6 1.1 copy-start.8
Sparse Core Ops, SparseCore 0:
  10.4 55.9 all-gather.8
  68.2 34.5 all-gather.10
  288.0 114.9 all-gather.12
  582.7 114.8 all-gather.14
  789.8 341.9 reduce-scatter.2
  1134.2 76.0 reduce-scatter.4
